TPU v7x, 32 devices: a whole 2x2x4 slice. The times are simulated.
32 devices in a mesh: head: 4 (over y, x), batch: 8 (over z, core).
Axes of the slice: x: 2, y: 2, z: 4, core: 2. Of those that a mesh axis runs over, the one named last changes fastest.
Arguments:
- hidden_in: bfloat16 [8, 256, 4096], P('batch', None, 'head')
- w_query: bfloat16 [4096, 4096], P('batch', 'head'), may hold values from -0.09375 to 0.09375
- w_key: bfloat16 [4096, 4096], P('batch', 'head'), may hold values from -0.09375 to 0.09375
- w_value: bfloat16 [4096, 4096], P('batch', 'head'), may hold values from -0.09375 to 0.09375
- w_beta: bfloat16 [4096, 32], P('batch', 'head'), may hold values from -0.09375 to 0.09375
- w_out: bfloat16 [4096, 4096], P('head', 'batch'), may hold values from -0.125 to 0.125
- mem_pos: int32 [8, 2, 64], P('batch'), may hold values from 0 to 127, as said below
- memory_in: float32 [8, 32, 128, 128], P('batch', 'head'), may hold values from -6 to 6
Outputs:
- hidden_out: bfloat16 [8, 256, 4096], P('batch', None, 'head')
- memory_out: float32 [8, 32, 128, 128], P('batch', 'head')
Inputs may be any that keep to these rules, and one draw needn't show every extreme that they name: `mem_pos`: within each sequence and segment the 64 positions are distinct and ascending.
All inputs are finite; a program needn't handle non-finite values.
Results may differ from a plain program's by a relative error of at most 0.005.
Values may be sent and summed in bfloat16 or wider, within the bound.
No kernel may reach another device: no remote copies, remote signals or barrier semaphores. Data moves between devices by JAX's collectives and lax.ppermute only.
A program may use at most 128 MiB of HBM per device.

v0:
```python
import jax
import jax.numpy as jnp
from jax import lax
from jax.sharding import PartitionSpec as P

SEGS = 2
epsilon = 1e-05


def recur(query, keys, values, beta, state):
    highest = lax.Precision.HIGHEST
    readouts = []
    for segment in range(query.shape[1]):
        readouts.append(
            jnp.einsum("bhij,blhj->blhi", state, query[:, segment], precision=highest).astype(
                jnp.bfloat16
            )
        )
        recalled = jnp.einsum("bhij,bmhj->bmhi", state, keys[:, segment], precision=highest)
        change = beta[:, segment][..., None] * (values[:, segment] - recalled)
        state = state + jnp.einsum("bmhi,bmhj->bhij", change, keys[:, segment], precision=highest)
    return (jnp.stack(readouts, axis=1), state)


def body(hidden_in, w_query, w_key, w_value, w_beta, w_out, mem_pos, memory_in):
    seq_count, row_count, local_width = hidden_in.shape
    seg_rows = row_count // SEGS
    mem_count = mem_pos.shape[2]
    local_heads = w_beta.shape[1]
    local_features = w_query.shape[1]
    head_size = local_features // local_heads
    x_float = hidden_in.astype(jnp.float32)
    whole = lax.all_gather(hidden_in, "head", axis=2, tiled=True)
    whole_float = whole.astype(jnp.float32)
    mean_square = jnp.mean(whole_float * whole_float, axis=2, keepdims=True)
    normed = (whole_float * lax.rsqrt(mean_square + epsilon)).astype(jnp.bfloat16)
    full_width = normed.shape[2]
    offsets = (jnp.arange(SEGS, dtype=jnp.int32) * seg_rows)[None, :, None]
    picked = (mem_pos + offsets).reshape(seq_count, SEGS * mem_count)
    memory_rows = jax.vmap(lambda block, where: jnp.take(block, where, axis=0))(normed, picked)
    memory_rows = memory_rows.reshape(seq_count * SEGS * mem_count, full_width)
    token_rows = normed.reshape(seq_count * row_count, full_width)
    piece_query = lax.all_gather(w_query, "batch", axis=0, tiled=True)
    piece_key = lax.all_gather(w_key, "batch", axis=0, tiled=True)
    piece_value = lax.all_gather(w_value, "batch", axis=0, tiled=True)
    piece_beta = lax.all_gather(w_beta, "batch", axis=0, tiled=True)
    query = jnp.dot(token_rows, piece_query, preferred_element_type=jnp.float32)
    keys = jnp.dot(memory_rows, piece_key, preferred_element_type=jnp.float32)
    values = jnp.dot(memory_rows, piece_value, preferred_element_type=jnp.float32)
    logits = jnp.dot(memory_rows, piece_beta, preferred_element_type=jnp.float32)
    query = (query * head_size ** (-0.5)).reshape(seq_count, SEGS, seg_rows, local_heads, head_size)
    keys = keys.reshape(seq_count, SEGS, mem_count, local_heads, head_size)
    keys = keys * lax.rsqrt(jnp.sum(keys * keys, axis=-1, keepdims=True) + 1e-06)
    values = values.reshape(seq_count, SEGS, mem_count, local_heads, head_size)
    beta = jax.nn.sigmoid(logits).reshape(seq_count, SEGS, mem_count, local_heads)
    readout, state = recur(query, keys, values, beta, memory_in)
    readout = readout.reshape(seq_count * row_count, local_features)
    terms = jnp.dot(
        readout,
        lax.all_gather(w_out, "batch", axis=1, tiled=True),
        preferred_element_type=jnp.float32,
    )
    mixed = lax.psum_scatter(terms, "head", scatter_dimension=1, tiled=True)
    hidden_out = (mixed + x_float.reshape(seq_count * row_count, local_width)).astype(jnp.bfloat16)
    return (hidden_out.reshape(hidden_in.shape), state)


def solution(mesh):
    in_specs = (
        P("batch", None, "head"),
        P("batch", "head"),
        P("batch", "head"),
        P("batch", "head"),
        P("batch", "head"),
        P("head", "batch"),
        P("batch", None, None),
        P("batch", "head", None, None),
    )
    out_specs = (P("batch", None, "head"), P("batch", "head", None, None))
    return jax.shard_map(body, mesh=mesh, in_specs=in_specs, out_specs=out_specs, check_vma=False)
```

profile of v0, /device:TPU:0, one launch (start us, length us, event | category | flops | bytes accessed | tf_op | source)
XLA Modules:
  0.0 445.6 jit_solution(10736198151364103323)
XLA Ops:
  10.6 0.8 broadcast_add_fusion
  11.5 15.9 %all_gather.20 = bf16[4096,8]{0,1:T(8,128)(2,1)S(1)} all-gather(bf16[512,8]{0,1:T(8,128)(2,1)} %param.12), channel_id=1, replica_groups=mesh['head'=4,'batch'=8] {'batch'}, dimensions={0}, use_global_device_ids=true | all-gather | bytes 73728 | tf_op jit(solution)/shard_map/all_gather | solution.py:46
  27.4 20.3 %all-gather.6.cloned.1.call-done = bf16[1,256,4096]{2,1,0:T(8,128)(2,1)} async-done(((bf16[1,256,1024]{2,1,0:T(8,128)(2,1)}), bf16[1,256,4096]{2,1,0:T(8,128)(2,1)}) %all-gather.6.cloned.1.call-update) | async-done | bytes 2097168 | tf_op jit(solution)/shard_map/all_gather | solution.py:33
  47.8 2.1 fusion
  49.8 2.2 fusion.1
  52.0 3.7 gather_fusion
  56.3 1.2 bitcast_select_fusion
  57.5 73.9 %all-gather.12.cloned.1.call-done = bf16[4096,1024]{1,0:T(8,128)(2,1)} async-done(((bf16[512,1024]{1,0:T(8,128)(2,1)}), bf16[4096,1024]{1,0:T(8,128)(2,1)}) %all-gather.12.cloned.1.call-update) | async-done | bytes 8388624 | tf_op jit(solution)/shard_map/all_gather | solution.py:44
  131.4 4.7 %convolution_bitcast_fusion.2 = f32[16,8,8,128]{3,1,2,0:T(8,128)S(1)} fusion(bf16[4096,1024]{1,0:T(8,128)(2,1)} %all-gather.12.cloned.1.call-done, bf16[128,4096]{1,0:T(8,128)(2,1)S(1)} %gather_fusion, pred[128]{0:T(512)(128)(4,1)S(1)} %compare_and_fusion), kind=kOutput, calls=%fused_computation.11 | convolution fusion | flops 1074266112 | bytes 9961600 | tf_op jit(solution)/shard_map/dot_general | solution.py:48
  136.5 77.1 %all-gather.10.cloned.1.call-done = bf16[4096,1024]{1,0:T(8,128)(2,1)} async-done(((bf16[512,1024]{1,0:T(8,128)(2,1)}), bf16[4096,1024]{1,0:T(8,128)(2,1)}) %all-gather.10.cloned.1.call-update) | async-done | bytes 8388624 | tf_op jit(solution)/shard_map/all_gather | solution.py:45
  213.6 12.1 %copy.27 = bf16[1024,4096]{1,0:T(8,128)(2,1)} copy(bf16[1024,4096]{0,1:T(8,128)(2,1)} %bitcast.131) | data formatting | bytes 16777216 | tf_op jit(solution)/shard_map/dot_general | solution.py:49
  225.7 69.9 %all-gather.8.cloned.1.call-done = bf16[4096,1024]{1,0:T(8,128)(2,1)} async-done(((bf16[512,1024]{1,0:T(8,128)(2,1)}), bf16[4096,1024]{1,0:T(8,128)(2,1)}) %all-gather.8.cloned.1.call-update) | async-done | bytes 8388624 | tf_op jit(solution)/shard_map/all_gather | solution.py:43
  295.6 5.9 %fusion.7 = f32[32,8,8,128]{3,1,2,0:T(8,128)S(1)} fusion(bf16[4096,1024]{1,0:T(8,128)(2,1)} %all-gather.8.cloned.1.call-done, bf16[1,256,4096]{2,1,0:T(8,128)(2,1)S(1)} %fusion.1), kind=kOutput, calls=%fused_computation.8 | convolution fusion | flops 2147745792 | bytes 11534336 | tf_op jit(solution)/shard_map/dot_general | solution.py:47
  301.7 1.2 fusion.12
  303.2 2.9 convolution_bitcast_fusion.3
  306.1 1.1 fusion.17
  307.2 1.0 fusion.10
  308.3 1.2 fusion.13
  309.9 67.7 %all-gather.14.cloned.1.call-done = bf16[1024,4096]{1,0:T(8,128)(2,1)} async-done(((bf16[1024,512]{1,0:T(8,128)(2,1)}), bf16[1024,4096]{1,0:T(8,128)(2,1)}) %all-gather.14.cloned.1.call-update) | async-done | bytes 8388624 | tf_op jit(solution)/shard_map/all_gather | solution.py:60
  377.6 7.7 %fusion.25 = f32[256,4096]{1,0:T(8,128)} fusion(bf16[1024,4096]{1,0:T(8,128)(2,1)} %all-gather.14.cloned.1.call-done, bf16[32,8,8,128]{3,2,1,0:T(8,128)(2,1)S(1)} %bitcast.136), kind=kOutput, calls=%fused_computation.36 | convolution fusion | flops 2147483648 | bytes 13107200 | tf_op jit(solution)/shard_map/dot_general | solution.py:58
  385.4 1.1 fusion.19
  386.5 1.8 fusion.11
  388.3 48.3 %reduce-scatter.2.cloned.1.call-done = f32[256,1024]{1,0:T(8,128)} async-done(((f32[256,4096]{1,0:T(8,128)}), f32[256,1024]{1,0:T(8,128)}) %reduce-scatter.2.cloned.1.call-update) | async-done | bytes 1048592 | tf_op jit(solution)/shard_map/reduce_scatter | solution.py:63
  436.6 2.2 fusion.24
  (40 shorter events, 5.4 us)
Async XLA Ops:
  7.2 40.6 %all-gather.6.cloned.1.call-start = ((), (), s32[]{:S(2)}) async-start(), calls=%async_computation.1 | async-start | bytes 2621440 | tf_op jit(solution)/shard_map/all_gather | solution.py:33
  7.9 123.5 %all-gather.12.cloned.1.call-start = ((), (), s32[]{:S(2)}) async-start(), calls=%async_computation.4 | async-start | bytes 9437184 | tf_op jit(solution)/shard_map/all_gather | solution.py:44
  8.6 204.9 %all-gather.10.cloned.1.call-start = ((), (), s32[]{:S(2)}) async-start(), calls=%async_computation.3 | async-start | bytes 9437184 | tf_op jit(solution)/shard_map/all_gather | solution.py:45
  9.4 286.2 %all-gather.8.cloned.1.call-start = ((), (), s32[]{:S(2)}) async-start(), calls=%async_computation.2 | async-start | bytes 9437184 | tf_op jit(solution)/shard_map/all_gather | solution.py:43
  10.0 367.6 %all-gather.14.cloned.1.call-start = ((), (), s32[]{:S(2)}) async-start(), calls=%async_computation.5 | async-start | bytes 9437184 | tf_op jit(solution)/shard_map/all_gather | solution.py:60
  10.5 426.0 %reduce-scatter.2.cloned.1.call-start = ((), (), s32[]{:S(2)}) async-start(), calls=%async_computation.6 | async-start | bytes 5242880 | tf_op jit(solution)/shard_map/reduce_scatter | solution.py:63
  225.7 76.1 %copy-start.1 = (f32[1,8,128,128]{3,2,1,0:T(8,128)S(1)}, f32[1,8,128,128]{3,2,1,0:T(8,128)}, u32[]{:S(2)}) copy-start(f32[1,8,128,128]{3,2,1,0:T(8,128)} %param.15) | copy-start | bytes 1572868
  295.6 7.6 %copy-start = (bf16[1024,4096]{1,0:T(8,128)(2,1)S(1)}, bf16[1024,4096]{1,0:T(8,128)(2,1)}, u32[]{:S(2)}) copy-start(bf16[1024,4096]{1,0:T(8,128)(2,1)} %copy.27) | copy-start | bytes 25165828
  295.6 7.6 %copy-start.2 = (bf16[1,128,1,1,1,1,4096]{6,1,5,4,3,2,0:T(8,128)(2,1)S(1)}, bf16[1,128,1,1,1,1,4096]{6,1,5,4,3,2,0:T(8,128)(2,1)}, u32[]{:S(2)}) copy-start(bf16[1,128,1,1,1,1,4096]{6,1,5,4,3,2,0:T(8,128)(2,1)} %bitcast_select_fusion) | copy-start | bytes 3145732
  377.6 59.0 %copy-start.3 = (bf16[1,256,1024]{2,1,0:T(8,128)(2,1)S(1)}, bf16[1,256,1024]{2,1,0:T(8,128)(2,1)}, u32[]{:S(2)}) copy-start(bf16[1,256,1024]{2,1,0:T(8,128)(2,1)} %param.8) | copy-start | bytes 1572868
Sparse Core Ops, SparseCore 0:
  9.8 37.8 all-gather.5
  49.3 82.0 all-gather.11
  133.0 80.5 all-gather.9
  215.0 80.5 all-gather.7
  297.0 80.5 all-gather.13
  385.5 51.0 reduce-scatter.1
where the time goes:
time: 446 us
  waiting for transfers between devices  360 us (81%)
  matrix products  29.1 us (7%)
  local copies, waits for them, and re-layouts  16.9 us (4%)
  blocking collectives  15.9 us (4%)
  between operations  14.3 us (3%)
  other arithmetic  8.83 us (2%)
    all_gather x1, waiting for transfers between devices, body(): piece_value = lax.all_gather(w_value, 'batch', axis=0, tiled=True)  77.1 us
    all_gather x1, waiting for transfers between devices, body(): piece_key = lax.all_gather(w_key, 'batch', axis=0, tiled=True)  73.9 us
    all_gather x1, waiting for transfers between devices, body(): piece_query = lax.all_gather(w_query, 'batch', axis=0, tiled=True)  69.9 us
    all_gather x1, waiting for transfers between devices, body(): lax.all_gather(w_out, 'batch', axis=1, tiled=True)  67.7 us
    reduce_scatter x1, waiting for transfers between devices, body(): mixed = lax.psum_scatter(terms, 'head', scatter_dimension=1, tiled=True)  48.3 us
    all_gather x1, waiting for transfers between devices, body(): whole = lax.all_gather(hidden_in, 'head', axis=2, tiled=True)  20.3 us
    all_gather x1, blocking collectives, body(): piece_beta = lax.all_gather(w_beta, 'batch', axis=0, tiled=True)  15.9 us
    dot_general x1, local copies, waits for them, and re-layouts, body(): jnp.dot(memory_rows, piece_value, preferred_element_type=jnp.float32)  12.1 us
  transfers between devices with their start and end apart: 6, of which 6 were waited for; matrix products, arithmetic and copies ran while one was open for 10% of the time, Pallas kernels for 0%

commit v1 on v0

--- a/solution.py
+++ b/solution.py
@@ -41,7 +41,11 @@
     memory_rows = memory_rows.reshape(seq_count * SEGS * mem_count, full_width)
     token_rows = normed.reshape(seq_count * row_count, full_width)
     piece_query = lax.all_gather(w_query, "batch", axis=0, tiled=True)
-    piece_key = lax.all_gather(w_key, "batch", axis=0, tiled=True)
+    size = lax.axis_size("batch")
+    repeats = [size if d == 0 else 1 for d in range(w_key.ndim)]
+    piece_key = lax.all_to_all(
+        jnp.tile(w_key, repeats), "batch", split_axis=0, concat_axis=0, tiled=True
+    )
     piece_value = lax.all_gather(w_value, "batch", axis=0, tiled=True)
     piece_beta = lax.all_gather(w_beta, "batch", axis=0, tiled=True)
     query = jnp.dot(token_rows, piece_query, preferred_element_type=jnp.float32)

time: 446 us -> 494 us (1.11)
  blocking collectives: 15.9 us -> 320 us
  waiting for transfers between devices: 360 us -> 89.7 us
  local copies, waits for them, and re-layouts: 16.9 us -> 24 us
  starting transfers between devices: 0.23 us -> 6.67 us
    all_gather x1, blocking collectives: 15.9 us -> 320 us  [body(): piece_beta = lax.all_gather(w_beta, 'batch', axis=0, tiled=True)]
    all_gather x1, waiting for transfers between devices: 77.1 us -> 0.01 us  [body(): piece_value = lax.all_gather(w_value, 'batch', axis=0, tiled=True)]
    all_gather x1 -> x0, waiting for transfers between devices: 73.9 us -> none  [body(): piece_key = lax.all_gather(w_key, 'batch', axis=0, tiled=True)]
    all_gather x1, waiting for transfers between devices: 69.9 us -> 0.01 us  [body(): piece_query = lax.all_gather(w_query, 'batch', axis=0, tiled=True)]
    all_gather x1, waiting for transfers between devices: 67.7 us -> 38.7 us  [body(): lax.all_gather(w_out, 'batch', axis=1, tiled=True)]
    all_gather x1, waiting for transfers between devices: 20.3 us -> 0.02 us  [body(): whole = lax.all_gather(hidden_in, 'head', axis=2, tiled=True)]
    all_to_all x0 -> x1, starting transfers between devices: none -> 6.49 us  [body(): lax.all_to_all(jnp.tile(w_key, repeats), 'batch', split_axis=0, concat_ax...]
    another operation x0 -> x1, local copies, waits for them, and re-layouts: none -> 5.53 us  [body(): jnp.tile(w_key, repeats)]
  transfers between devices with their start and end apart: 6 -> 6, of which waited for: 6 -> 2; matrix products, arithmetic and copies ran while one was open for 10% -> 11% of each run, Pallas kernels for 0% -> 0%
where the time goes in v1:
time: 494 us; the launch traced here: 493 us
  blocking collectives  320 us (65%)
  waiting for transfers between devices  89.7 us (18%)
  matrix products  30.5 us (6%)
  local copies, waits for them, and re-layouts  24 us (5%)
  between operations  14 us (3%)
  other arithmetic  8.45 us (2%)
  starting transfers between devices  6.67 us (1%)
    all_gather x1, blocking collectives, body(): piece_beta = lax.all_gather(w_beta, 'batch', axis=0, tiled=True)  320 us
    reduce_scatter x1, waiting for transfers between devices, body(): mixed = lax.psum_scatter(terms, 'head', scatter_dimension=1, tiled=True)  48.3 us
    all_gather x1, waiting for transfers between devices, body(): lax.all_gather(w_out, 'batch', axis=1, tiled=True)  38.7 us
    dot_general x1, local copies, waits for them, and re-layouts, body(): jnp.dot(memory_rows, piece_value, preferred_element_type=jnp.float32)  11.8 us
  transfers between devices with their start and end apart: 6, of which 2 were waited for; matrix products, arithmetic and copies ran while one was open for 11% of the time, Pallas kernels for 0%

profile of v1, /device:TPU:0, one launch (start us, length us, event | category | flops | bytes accessed | tf_op | source)
XLA Modules:
  0.0 493.0 jit_solution(11289746915705233616)
XLA Ops:
  7.9 0.7 all-gather.9.cloned.1.call-update
  9.4 5.5 %tile.2 = bf16[8,512,1024]{2,1,0:T(8,128)(2,1)} broadcast(bf16[512,1024]{1,0:T(8,128)(2,1)} %param.10), dimensions={1,2} | broadcast | bytes 9437184 | tf_op jit(solution)/shard_map/tile | solution.py:47
  14.9 6.5 %all-to-all-start = ((bf16[8,512,1024]{2,1,0:T(8,128)(2,1)}), bf16[8,512,1024]{2,1,0:T(8,128)(2,1)}, u32[]{:S(2)}, u32[]{:S(2)}) async-start(bf16[8,512,1024]{2,1,0:T(8,128)(2,1)} %tile.2), calls=%async_computation | async-start | bytes 16777216 | tf_op jit(solution)/shard_map/all_to_all | solution.py:46
  22.3 319.7 %all_gather.17 = bf16[4096,8]{0,1:T(8,128)(2,1)S(1)} all-gather(bf16[512,8]{0,1:T(8,128)(2,1)S(1)} %copy-done.5), channel_id=1, replica_groups=mesh['head'=4,'batch'=8] {'batch'}, dimensions={0}, use_global_device_ids=true | all-gather | bytes 73728 | tf_op jit(solution)/shard_map/all_gather | solution.py:50
  342.1 2.1 fusion
  344.2 2.2 fusion.1
  346.4 4.7 gather_fusion
  351.1 1.8 fusion.22
  353.0 1.5 bitcast_select_fusion
  354.4 4.6 convolution_bitcast_fusion.2
  359.2 0.8 copy-done.2
  360.3 11.8 %copy.27 = bf16[1024,4096]{1,0:T(8,128)(2,1)} copy(bf16[1024,4096]{0,1:T(8,128)(2,1)} %bitcast.136) | data formatting | bytes 16777216 | tf_op jit(solution)/shard_map/dot_general | solution.py:53
  372.1 5.9 %fusion.7 = f32[32,8,8,128]{3,1,2,0:T(8,128)S(1)} fusion(bf16[4096,1024]{1,0:T(8,128)(2,1)} %all-gather.7.cloned.1.call-done, bf16[1,256,4096]{2,1,0:T(8,128)(2,1)S(1)} %fusion.1), kind=kOutput, calls=%fused_computation.8 | convolution fusion | flops 2147745792 | bytes 11534336 | tf_op jit(solution)/shard_map/dot_general | solution.py:51
  378.4 1.3 fusion.12
  379.9 2.9 convolution_bitcast_fusion.3
  382.7 1.1 fusion.17
  383.9 1.0 fusion.10
  384.9 1.2 fusion.13
  386.5 38.7 %all-gather.11.cloned.1.call-done = bf16[1024,4096]{1,0:T(8,128)(2,1)} async-done(((bf16[1024,512]{1,0:T(8,128)(2,1)}), bf16[1024,4096]{1,0:T(8,128)(2,1)}) %all-gather.11.cloned.1.call-update) | async-done | bytes 8388624 | tf_op jit(solution)/shard_map/all_gather | solution.py:64
  425.3 7.7 %fusion.28 = f32[256,4096]{1,0:T(8,128)} fusion(bf16[1024,4096]{1,0:T(8,128)(2,1)} %all-gather.11.cloned.1.call-done, bf16[32,8,8,128]{3,2,1,0:T(8,128)(2,1)S(1)} %bitcast.140), kind=kOutput, calls=%fused_computation.38 | convolution fusion | flops 2147483648 | bytes 13107200 | tf_op jit(solution)/shard_map/dot_general | solution.py:62
  433.0 1.1 fusion.19
  434.2 1.8 fusion.11
  436.0 48.3 %reduce-scatter.2.cloned.1.call-done = f32[256,1024]{1,0:T(8,128)} async-done(((f32[256,4096]{1,0:T(8,128)}), f32[256,1024]{1,0:T(8,128)}) %reduce-scatter.2.cloned.1.call-update) | async-done | bytes 1048592 | tf_op jit(solution)/shard_map/reduce_scatter | solution.py:67
  484.3 2.2 fusion.27
  (46 shorter events, 3.8 us)
Async XLA Ops:
  7.2 334.9 %all-gather.5.cloned.1.call-start = ((), (), s32[]{:S(2)}) async-start(), calls=%async_computation.2 | async-start | bytes 2621440 | tf_op jit(solution)/shard_map/all_gather | solution.py:33
  7.9 352.4 %all-gather.9.cloned.1.call-start = ((), (), s32[]{:S(2)}) async-start(), calls=%async_computation.4 | async-start | bytes 9437184 | tf_op jit(solution)/shard_map/all_gather | solution.py:49
  8.6 363.5 %all-gather.7.cloned.1.call-start = ((), (), s32[]{:S(2)}) async-start(), calls=%async_computation.3 | async-start | bytes 9437184 | tf_op jit(solution)/shard_map/all_gather | solution.py:43
  14.9 7.1 %copy-start.6 = (s32[1,2,64]{2,1,0:T(2,128)S(1)}, s32[1,2,64]{2,1,0:T(2,128)}, u32[]{:S(2)}) copy-start(s32[1,2,64]{2,1,0:T(2,128)} %param.14) | copy-start | bytes 1540
  14.9 7.4 %copy-start.5 = (bf16[512,8]{0,1:T(8,128)(2,1)S(1)}, bf16[512,8]{0,1:T(8,128)(2,1)}, u32[]{:S(2)}) copy-start(bf16[512,8]{0,1:T(8,128)(2,1)} %param.12) | copy-start | bytes 24580
  14.9 339.5 %all-to-all-start = ((bf16[8,512,1024]{2,1,0:T(8,128)(2,1)}), bf16[8,512,1024]{2,1,0:T(8,128)(2,1)}, u32[]{:S(2)}, u32[]{:S(2)}) async-start(bf16[8,512,1024]{2,1,0:T(8,128)(2,1)} %tile.2), calls=%async_computation | async-start | bytes 16777216 | tf_op jit(solution)/shard_map/all_to_all | solution.py:46
  21.4 403.9 %all-gather.11.cloned.1.call-start = ((), (), s32[]{:S(2)}) async-start(), calls=%async_computation.5 | async-start | bytes 9437184 | tf_op jit(solution)/shard_map/all_gather | solution.py:64
  22.0 462.3 %reduce-scatter.2.cloned.1.call-start = ((), (), s32[]{:S(2)}) async-start(), calls=%async_computation.6 | async-start | bytes 5242880 | tf_op jit(solution)/shard_map/reduce_scatter | solution.py:67
  359.2 0.8 copy-start.2
  372.1 6.2 %copy-start.1 = (f32[1,8,128,128]{3,2,1,0:T(8,128)S(1)}, f32[1,8,128,128]{3,2,1,0:T(8,128)}, u32[]{:S(2)}) copy-start(f32[1,8,128,128]{3,2,1,0:T(8,128)} %param.15) | copy-start | bytes 1572868
  372.1 7.5 %copy-start.3 = (f32[16,8,8,128]{3,2,1,0:T(8,128)S(1)}, f32[16,8,8,128]{3,2,1,0:T(8,128)}, u32[]{:S(2)}) copy-start(f32[16,8,8,128]{3,2,1,0:T(8,128)} %copy-done.2) | copy-start | bytes 1572868
  372.1 7.7 %copy-start = (bf16[1024,4096]{1,0:T(8,128)(2,1)S(1)}, bf16[1024,4096]{1,0:T(8,128)(2,1)}, u32[]{:S(2)}) copy-start(bf16[1024,4096]{1,0:T(8,128)(2,1)} %copy.27) | copy-start | bytes 25165828
  425.3 59.0 %copy-start.4 = (bf16[1,256,1024]{2,1,0:T(8,128)(2,1)S(1)}, bf16[1,256,1024]{2,1,0:T(8,128)(2,1)}, u32[]{:S(2)}) copy-start(bf16[1,256,1024]{2,1,0:T(8,128)(2,1)} %param.8) | copy-start | bytes 1572868
Sparse Core Ops, SparseCore 0:
  9.8 37.8 all-gather.4
  49.4 187.8 all-gather.8
  238.8 103.8 all-gather.6
  344.2 81.0 all-gather.10
  433.2 51.0 reduce-scatter.1
